TPU v7x, 32 devices: a whole 2x2x4 slice. The times are simulated.
32 devices in a mesh: groups: 2 (over x), grid: 4 (over y, core), chol: 4 (over z).
Axes of the slice: x: 2, y: 2, z: 4, core: 2. Of those that a mesh axis runs over, the one named last changes fastest.
Arguments:
- chol_block: float32 [8, 1024, 1024], P(('groups', 'chol'), 'grid'), parts along dimension 0, may hold values from -6 to 6
- orbitals: float32 [8192, 1024], P(('groups', 'grid')), parts along dimension 0, may hold values from -0.1875 to 0.1875
- fit_in: float32 [8192, 4096], P(('groups', 'chol'), 'grid'), parts along dimension 0, may hold values from -6 to 6
Outputs:
- fit_out: float32 [8192, 4096], P(('groups', 'chol'), 'grid'), parts along dimension 0
There are 2 independent parts, one for each index of `groups`. A program takes and returns all parts, laid end to end along the dimension named above; each array names one. Nothing has to cross between parts.
All inputs are finite; a program needn't handle non-finite values.
Results may differ from a plain program's by a relative error of at most 0.000096.
Values sent between devices are 32-bit elements; how exact they have to be, the bound alone decides.
A program may use at most 64 MiB of HBM per device.

v0:
```python
import jax
import jax.numpy as jnp
from jax import lax
from jax.sharding import PartitionSpec as P


def on_device(chol_block, orbitals, fit_in):
    partial_half = jnp.einsum(
        "pr,vrq->vpq",
        orbitals,
        lax.all_gather(chol_block, "grid", axis=1, tiled=True),
        precision=lax.Precision.HIGHEST,
    )
    summed = jnp.einsum("vpq,pq->vp", partial_half, orbitals, precision=lax.Precision.HIGHEST)
    contracted = jnp.transpose(summed)
    tile_rows = fit_in.shape[0]
    widened = lax.all_gather(contracted, "chol", axis=1, tiled=True)
    everyone = lax.all_gather(widened, "grid", axis=0, tiled=True)
    own_rows = lax.dynamic_slice_in_dim(everyone, lax.axis_index("chol") * tile_rows, tile_rows, 0)
    fit_tile = jnp.dot(own_rows, jnp.transpose(widened), precision=lax.Precision.HIGHEST)
    return fit_in + fit_tile


def solution(mesh):
    placed = (
        P(("groups", "chol"), "grid", None),
        P(("groups", "grid"), None),
        P(("groups", "chol"), "grid"),
    )
    return jax.shard_map(
        on_device,
        mesh=mesh,
        in_specs=placed,
        out_specs=P(("groups", "chol"), "grid"),
        check_vma=False,
    )
```

profile of v0, /device:TPU:0, one launch (start us, length us, event | category | flops | bytes accessed | tf_op | source)
XLA Modules:
  0.0 116.4 jit_solution(9180656341693434953)
XLA Ops:
  6.5 0.0 all-gather.3.cloned.1.call-start
  6.5 0.7 all-gather.3.cloned.1.call-update
  7.3 38.9 %all-gather.3.cloned.1.call-done = f32[1,1024,1024]{2,1,0:T(8,128)} async-done(((f32[1,256,1024]{2,1,0:T(8,128)}), f32[1,1024,1024]{2,1,0:T(8,128)}) %all-gather.3.cloned.1.call-update) | async-done | bytes 4194320 | tf_op jit(solution)/shard_map/all_gather | solution.py:11
  46.1 30.4 %fusion.2 = f32[1024,1024]{0,1:T(8,128)} fusion(f32[1024,1024]{1,0:T(8,128)} %param.4, f32[1,1024,1024]{2,1,0:T(8,128)} %all-gather.3.cloned.1.call-done), kind=kOutput, calls=%fused_computation.3 | convolution fusion | flops 12884901888 | bytes 12582912 | tf_op jit(solution)/shard_map/pr,vrq->vpq/dot_general | solution.py:8
  76.6 5.3 %copy.7 = f32[1024,1024]{1,0:T(8,128)} copy(f32[1024,1024]{0,1:T(8,128)} %fusion.2) | data formatting | bytes 8388608
  81.9 0.0 copy-start
  81.9 4.0 %multiply_reduce_fusion = f32[1024]{0:T(1024)S(1)} fusion(f32[1024,1024]{1,0:T(8,128)} %copy.7, f32[1024,1024]{1,0:T(8,128)} %param.4), kind=kLoop, calls=%fused_computation.2 | loop fusion | flops 2096128 | bytes 8392704 | tf_op jit(solution)/shard_map/vpq,pq->vp/dot_general | solution.py:14
  86.0 13.2 %all-gather = f32[4,1,1024]{2,1,0:T(1,128)S(1)} all-gather(f32[1,1,1024]{2,1,0:T(1,128)S(1)} %bitcast.21), channel_id=1, replica_groups=mesh['groups'=2,'grid'=4,'chol'=4] {'chol'}, dimensions={0}, use_global_device_ids=true | all-gather | bytes 20480 | tf_op jit(solution)/shard_map/all_gather | solution.py:17
  99.1 5.2 %all_gather.11 = f32[4096,4]{0,1:T(4,128)S(1)} all-gather(f32[1024,4]{0,1:T(4,128)S(1)} %bitcast.20), channel_id=1, replica_groups=mesh['groups'=2,'grid'=4,'chol'=4] {'grid'}, dimensions={0}, use_global_device_ids=true | all-gather | bytes 81920 | tf_op jit(solution)/shard_map/all_gather | solution.py:18
  104.4 0.0 copy-done
  104.4 5.2 %convolution_add_fusion = f32[1024,1024]{1,0:T(8,128)} fusion(f32[1024,1024]{1,0:T(8,128)S(1)} %copy-done, f32[4096,4]{0,1:T(4,128)S(1)} %all_gather.11, s32[]{:T(128)S(6)} %select_n.3, f32[4,1,1024]{2,1,0:T(1,128)S(1)} %all-gather), kind=kOutput, calls=%fused_computation.4 | convolution fusion | flops 51380224 | bytes 8421380 | tf_op jit(solution)/shard_map/dot_general | solution.py:20
  (1 shorter events, 0.0 us)
Async XLA Ops:
  6.5 39.6 %all-gather.3.cloned.1.call-start = ((), (), s32[]{:S(2)}) async-start(), calls=%async_computation | async-start | bytes 5242880 | tf_op jit(solution)/shard_map/all_gather | solution.py:11
  81.9 22.5 %copy-start = (f32[1024,1024]{1,0:T(8,128)S(1)}, f32[1024,1024]{1,0:T(8,128)}, u32[]{:S(2)}) copy-start(f32[1024,1024]{1,0:T(8,128)} %param.5) | copy-start | bytes 12582916
Sparse Core Ops, SparseCore 0:
  8.9 37.1 all-gather.2
where the time goes:
time: 117 us; the launch traced here: 116 us
  waiting for transfers between devices  39.6 us (34%)
  matrix products  35.6 us (30%)
  blocking collectives  18.4 us (16%)
  between operations  13.4 us (11%)
  local copies, waits for them, and re-layouts  5.36 us (5%)
  other arithmetic  4.04 us (3%)
    all_gather x1, waiting for transfers between devices, on_device(): lax.all_gather(chol_block, 'grid', axis=1, tiled=True)  38.9 us
    dot_general x1, matrix products, on_device(): jnp.einsum('pr,vrq->vpq', orbitals, lax.all_gather(chol_block, 'grid', ax...  30.4 us
    all_gather x1, blocking collectives, on_device(): widened = lax.all_gather(contracted, 'chol', axis=1, tiled=True)  13.2 us
    unnamed x4, local copies, waits for them, and re-layouts  5.36 us
    all_gather x1, blocking collectives, on_device(): everyone = lax.all_gather(widened, 'grid', axis=0, tiled=True)  5.23 us
    dot_general x1, matrix products, on_device(): jnp.dot(own_rows, jnp.transpose(widened), precision=lax.Precision.HIGHEST)  5.2 us
    dot_general x1, other arithmetic, on_device(): jnp.einsum('vpq,pq->vp', partial_half, orbitals, precision=lax.Precision....  4.04 us
  transfers between devices with their start and end apart: 1, of which 1 were waited for; matrix products, arithmetic and copies ran while one was open for 0% of the time, Pallas kernels for 0%

commit v1 on v0

v1 whole, which is shorter than its diff:
```python
import functools

import jax
import jax.numpy as jnp
from jax import lax
from jax.experimental import pallas as pl
from jax.experimental.pallas import tpu as pltpu
from jax.sharding import PartitionSpec as P

MESH = pl.DeviceIdType.MESH
F32 = jnp.float32
BF16 = jnp.bfloat16


def split2(a):
    hi = a.astype(BF16)
    return hi, (a - hi.astype(F32)).astype(BF16)


def dot(a, b):
    return jnp.dot(a, b, preferred_element_type=F32)


def gather_kernel(ng, nc, nch, chol_hbm, orb_hbm, lhs_ref, rhs_ref,
                  lbuf, xbuf, xt, xth, xtl, acc, allc,
                  own_sem, x_sem, ysend, yrecv, ssend, srecv, csend, crecv):
    g = lax.axis_index("groups")
    i = lax.axis_index("grid")
    c = lax.axis_index("chol")
    rows, norb = lbuf.shape[1], lbuf.shape[2]
    pts = allc.shape[2]
    total = ng * nc
    chips = ng // 2
    core = lax.rem(i, 2)
    chip = lax.div(i, 2)
    sib = i + 1 - 2 * core
    flat = i * nc + c
    step = rows // nch

    own = pltpu.make_async_copy(chol_hbm.at[0], lbuf.at[i], own_sem)
    own.start()
    xcopy = pltpu.make_async_copy(orb_hbm, xbuf, x_sem)
    xcopy.start()

    barrier = pltpu.get_barrier_semaphore()
    for k in range(1, total):
        t = lax.rem(flat + k, total)
        pl.semaphore_signal(barrier, inc=1, device_id=(g, lax.div(t, nc), lax.rem(t, nc)), device_id_type=MESH)
    pl.semaphore_wait(barrier, total - 1)

    def chip_copy(ch, d):
        part = pl.ds(ch * step, step)
        to = lax.rem(chip + d, chips) * 2 + core
        return pltpu.make_async_remote_copy(
            src_ref=chol_hbm.at[0, part], dst_ref=lbuf.at[i, part],
            send_sem=ysend.at[ch, d], recv_sem=yrecv.at[ch, d],
            device_id=(g, to, c), device_id_type=MESH)

    def from_chip(ch, d):
        part = pl.ds(ch * step, step)
        src = lax.rem(chip - d + chips, chips) * 2 + core
        return src, pltpu.make_async_remote_copy(
            src_ref=lbuf.at[src, part], dst_ref=lbuf.at[src, part],
            send_sem=ysend.at[ch, d], recv_sem=yrecv.at[ch, d],
            device_id=(g, src, c), device_id_type=MESH)

    def forward(ch, d, src):
        part = pl.ds(ch * step, step)
        return pltpu.make_async_remote_copy(
            src_ref=lbuf.at[src, part], dst_ref=lbuf.at[src, part],
            send_sem=ssend.at[ch, d], recv_sem=srecv.at[ch, d],
            device_id=(g, sib, c), device_id_type=MESH)

    for ch in range(nch):
        for d in range(1, chips):
            chip_copy(ch, d).start()
    home = pltpu.make_async_remote_copy(
        src_ref=chol_hbm.at[0], dst_ref=lbuf.at[i],
        send_sem=ssend.at[0, 0], recv_sem=srecv.at[0, 0],
        device_id=(g, sib, c), device_id_type=MESH)
    home.start()

    xcopy.wait()
    tile = min(256, pts)

    @pl.loop(0, pts // tile)
    def _(p):
        at = pl.multiple_of(p * tile, tile)
        block = jnp.transpose(xbuf[pl.ds(at, tile), :])
        xt[:, pl.ds(at, tile)] = block
        hi, lo = split2(block)
        xth[:, pl.ds(at, tile)] = hi
        xtl[:, pl.ds(at, tile)] = lo

    acc[...] = jnp.zeros_like(acc)

    def add(src, first, count):
        hi, lo = split2(lbuf[src, pl.ds(first, count), :])
        base = pl.multiple_of(src * rows + first, 16)

        @pl.loop(0, pts // tile)
        def _(p):
            at = pl.multiple_of(p * tile, tile)
            cols = pl.ds(at, tile)
            half = dot(hi, xth[:, cols]) + (dot(lo, xth[:, cols]) + dot(hi, xtl[:, cols]))
            prod = half * xt[pl.ds(base, count), cols]
            acc[:, cols] += jnp.sum(prod.reshape(count // 8, 8, tile), axis=0)

    own.wait()
    add(i, 0, rows)
    home.wait()
    add(sib, 0, rows)

    for ch in range(nch):
        for d in range(1, chips):
            src, landed = from_chip(ch, d)
            landed.wait_recv()
            fwd = forward(ch, d, src)
            fwd.start()
            add(src, ch * step, step)
            fwd.wait_recv()
            add(src + 1 - 2 * core, ch * step, step)

    allc[flat] = jnp.sum(acc[...], axis=0, keepdims=True)

    def spread(k):
        t = lax.rem(flat + k, total)
        return pltpu.make_async_remote_copy(
            src_ref=allc.at[flat], dst_ref=allc.at[flat],
            send_sem=csend.at[k], recv_sem=crecv.at[k],
            device_id=(g, lax.div(t, nc), lax.rem(t, nc)), device_id_type=MESH)

    for k in range(1, total):
        spread(k).start()
    for ch in range(nch):
        for d in range(1, chips):
            src, _ = from_chip(ch, d)
            chip_copy(ch, d).wait_send()
            forward(ch, d, src).wait_send()
    for k in range(1, total):
        back = lax.rem(flat - k + total, total)
        pltpu.make_async_remote_copy(
            src_ref=allc.at[back], dst_ref=allc.at[back],
            send_sem=csend.at[k], recv_sem=crecv.at[k],
            device_id=(g, i, c), device_id_type=MESH).wait_recv()

    def terms(v):
        h = v.astype(BF16).astype(F32)
        r = v - h
        m = r.astype(BF16).astype(F32)
        return h, m, (r - m).astype(BF16).astype(F32)

    lhs_ref[...] = jnp.zeros_like(lhs_ref)
    rhs_ref[...] = jnp.zeros_like(rhs_ref)
    blocks = lhs_ref.shape[1] // pts
    for n in range(nc):
        h, m, l = terms(allc[i * nc + n])
        for t, v in enumerate((h, m, h, l, h, m)):
            rhs_ref[t * nc + n:t * nc + n + 1, :] = v
        for b in range(blocks):
            h, m, l = terms(allc[(c * blocks + b) * nc + n])
            for t, v in enumerate((h, h, m, h, l, m)):
                lhs_ref[t * nc + n:t * nc + n + 1, b * pts:(b + 1) * pts] = v
    for k in range(1, total):
        spread(k).wait_send()


def fit_kernel(lhs_ref, rhs_ref, fit_ref, out_ref):
    left = jnp.transpose(lhs_ref[...]).astype(BF16)
    out_ref[...] = fit_ref[...] + dot(left, rhs_ref[...].astype(BF16))


def on_device(ng, nc, chol_block, orbitals, fit_in):
    rows, norb = chol_block.shape[1:]
    pts = orbitals.shape[0]
    tile_rows, tile_cols = fit_in.shape
    nch = 4
    chips = ng // 2
    depth = -(-6 * nc // 8) * 8
    total = ng * nc
    dma = pltpu.SemaphoreType.DMA
    vmem = pl.BlockSpec(memory_space=pltpu.VMEM)
    hbm = pl.BlockSpec(memory_space=pl.ANY)
    lhs, rhs = pl.pallas_call(
        functools.partial(gather_kernel, ng, nc, nch),
        out_shape=(jax.ShapeDtypeStruct((depth, tile_rows), F32),
                   jax.ShapeDtypeStruct((depth, tile_cols), F32)),
        in_specs=[hbm, hbm],
        out_specs=(vmem, vmem),
        scratch_shapes=[
            pltpu.VMEM((ng, rows, norb), F32),
            pltpu.VMEM((pts, norb), F32),
            pltpu.VMEM((norb, pts), F32),
            pltpu.VMEM((norb, pts), BF16),
            pltpu.VMEM((norb, pts), BF16),
            pltpu.VMEM((8, pts), F32),
            pltpu.VMEM((total, 1, pts), F32),
            dma, dma,
            dma((nch, chips)), dma((nch, chips)),
            dma((nch, chips)), dma((nch, chips)),
            dma((total,)), dma((total,)),
        ],
        compiler_params=pltpu.CompilerParams(
            collective_id=0, has_side_effects=True, vmem_limit_bytes=40 << 20),
        name="gather",
    )(chol_block, orbitals)
    tile = min(256, tile_rows)
    return pl.pallas_call(
        fit_kernel,
        grid=(tile_rows // tile,),
        out_shape=jax.ShapeDtypeStruct(fit_in.shape, F32),
        in_specs=[
            pl.BlockSpec((depth, tile), lambda r: (0, r)),
            pl.BlockSpec((depth, tile_cols), lambda r: (0, 0)),
            pl.BlockSpec((tile, tile_cols), lambda r: (r, 0)),
        ],
        out_specs=pl.BlockSpec((tile, tile_cols), lambda r: (r, 0)),
        name="fit",
    )(lhs, rhs, fit_in)


def solution(mesh):
    placed = (
        P(("groups", "chol"), "grid", None),
        P(("groups", "grid"), None),
        P(("groups", "chol"), "grid"),
    )
    return jax.shard_map(
        functools.partial(on_device, mesh.shape["grid"], mesh.shape["chol"]),
        mesh=mesh,
        in_specs=placed,
        out_specs=P(("groups", "chol"), "grid"),
        check_vma=False,
    )
```

time: 117 us -> 48.3 us (0.41)
  Pallas kernels: 0 us -> 43.3 us
  waiting for transfers between devices: 39.6 us -> 0 us
  matrix products: 35.6 us -> 0 us
  blocking collectives: 18.4 us -> 0 us
  between operations: 13.4 us -> 0.02 us
  other arithmetic: 4.04 us -> 0 us
    pallas_call x0 -> x2, Pallas kernels: none -> 43.3 us  [the longest x1 38 us: on_device(): pl.pallas_call(functools.partial(gather_kernel, ng, nc, nch), out_shape=(...]
    all_gather x1 -> x0, waiting for transfers between devices: 38.9 us -> none  [on_device(): lax.all_gather(chol_block, 'grid', axis=1, tiled=True)]
    dot_general x2 -> x0, matrix products: 35.6 us -> none  [the longest x1 30.4 us: on_device(): jnp.einsum('pr,vrq->vpq', orbitals, lax.all_gather(chol_block, 'grid', ax...]
    all_gather x2 -> x0, blocking collectives: 18.4 us -> none  [the longest x1 13.2 us: on_device(): widened = lax.all_gather(contracted, 'chol', axis=1, tiled=True)]
    dot_general x1 -> x0, other arithmetic: 4.04 us -> none  [on_device(): jnp.einsum('vpq,pq->vp', partial_half, orbitals, precision=lax.Precision....]
    unnamed x4 -> x8, local copies, waits for them, and re-layouts: 5.36 us -> 4.68 us
  transfers between devices with their start and end apart: 1 -> 0, of which waited for: 1 -> 0; matrix products, arithmetic and copies ran while one was open for 0% -> 0% of each run, Pallas kernels for 0% -> 0%
where the time goes in v1:
time: 48.3 us; the launch traced here: 48 us
  Pallas kernels  43.3 us (90%)
  local copies, waits for them, and re-layouts  4.68 us (10%)
    pallas_call x1, Pallas kernels, on_device(): pl.pallas_call(functools.partial(gather_kernel, ng, nc, nch), out_shape=(...  38 us
    pallas_call x1, Pallas kernels, on_device(): pl.pallas_call(fit_kernel, grid=(tile_rows // tile,), out_shape=jax.Shape...  5.27 us
    unnamed x8, local copies, waits for them, and re-layouts  4.68 us

profile of v1, /device:TPU:0, one launch (start us, length us, event | category | flops | bytes accessed | tf_op | source)
XLA Modules:
  0.0 48.0 jit_solution(16834065317704080748)
XLA Ops:
  0.0 0.0 copy-start
  0.0 2.2 %copy-done = f32[1024,1024]{1,0:T(8,128)S(1)} copy-done((f32[1024,1024]{1,0:T(8,128)S(1)}, f32[1024,1024]{1,0:T(8,128)}, u32[]{:S(2)}) %copy-start) | copy-done | bytes 4194328
  2.2 0.0 copy-start.1
  2.2 1.2 %copy-done.1 = f32[1,256,1024]{2,1,0:T(8,128)S(1)} copy-done((f32[1,256,1024]{2,1,0:T(8,128)S(1)}, f32[1,256,1024]{2,1,0:T(8,128)}, u32[]{:S(2)}) %copy-start.1) | copy-done | bytes 1048600
  3.4 38.0 %gather.1 = (f32[24,1024]{1,0:T(8,128)S(1)}, f32[24,1024]{1,0:T(8,128)S(1)}) custom-call(f32[1,256,1024]{2,1,0:T(8,128)S(1)} %copy-done.1, f32[1024,1024]{1,0:T(8,128)S(1)} %copy-done), custom_call_target="tpu_custom_call" | custom-call | tf_op jit(solution)/shard_map/gather/pallas_call | solution.py:184
  41.4 0.0 copy-start.2
  41.4 0.6 %copy-done.2 = f32[24,1024]{1,0:T(8,128)} copy-done((f32[24,1024]{1,0:T(8,128)}, f32[24,1024]{1,0:T(8,128)S(1)}, u32[]{:S(2)}) %copy-start.2) | copy-done | bytes 98328
  42.1 0.0 copy-start.3
  42.1 0.6 %copy-done.3 = f32[24,1024]{1,0:T(8,128)} copy-done((f32[24,1024]{1,0:T(8,128)}, f32[24,1024]{1,0:T(8,128)S(1)}, u32[]{:S(2)}) %copy-start.3) | copy-done | bytes 98328
  42.7 5.3 %fit.1 = f32[1024,1024]{1,0:T(8,128)} custom-call(f32[24,1024]{1,0:T(8,128)} %copy-done.2, f32[24,1024]{1,0:T(8,128)} %copy-done.3, f32[1024,1024]{1,0:T(8,128)} %fit_ref.1), custom_call_target="tpu_custom_call" | custom-call | tf_op jit(solution)/shard_map/fit/pallas_call | solution.py:208
Async XLA Ops:
  0.0 2.2 %copy-start = (f32[1024,1024]{1,0:T(8,128)S(1)}, f32[1024,1024]{1,0:T(8,128)}, u32[]{:S(2)}) copy-start(f32[1024,1024]{1,0:T(8,128)} %orb_hbm.1) | copy-start | bytes 12582916
  2.2 1.2 %copy-start.1 = (f32[1,256,1024]{2,1,0:T(8,128)S(1)}, f32[1,256,1024]{2,1,0:T(8,128)}, u32[]{:S(2)}) copy-start(f32[1,256,1024]{2,1,0:T(8,128)} %chol_hbm.1) | copy-start | bytes 3145732
  41.4 0.6 %copy-start.2 = (f32[24,1024]{1,0:T(8,128)}, f32[24,1024]{1,0:T(8,128)S(1)}, u32[]{:S(2)}) copy-start(f32[24,1024]{1,0:T(8,128)S(1)} %get-tuple-element.7.lhs_ref) | copy-start | bytes 294916
  42.1 0.6 %copy-start.3 = (f32[24,1024]{1,0:T(8,128)}, f32[24,1024]{1,0:T(8,128)S(1)}, u32[]{:S(2)}) copy-start(f32[24,1024]{1,0:T(8,128)S(1)} %get-tuple-element.8.rhs_ref) | copy-start | bytes 294916

commit v2 on v1

--- a/solution.py
+++ b/solution.py
@@ -21,9 +21,9 @@
     return jnp.dot(a, b, preferred_element_type=F32)
 
 
-def gather_kernel(ng, nc, nch, chol_hbm, orb_hbm, lhs_ref, rhs_ref,
+def gather_kernel(ng, nc, nch, chol_hbm, orb_hbm, fit_hbm, lhs_ref, rhs_ref, held_ref,
                   lbuf, xbuf, xt, xth, xtl, acc, allc,
-                  own_sem, x_sem, ysend, yrecv, ssend, srecv, csend, crecv):
+                  own_sem, x_sem, fit_sem, ysend, yrecv, ssend, srecv, csend, crecv):
     g = lax.axis_index("groups")
     i = lax.axis_index("grid")
     c = lax.axis_index("chol")
@@ -81,6 +81,8 @@
     home.start()
 
     xcopy.wait()
+    keep = pltpu.make_async_copy(fit_hbm, held_ref, fit_sem)
+    keep.start()
     tile = min(256, pts)
 
     @pl.loop(0, pts // tile)
@@ -163,11 +165,21 @@
                 lhs_ref[t * nc + n:t * nc + n + 1, b * pts:(b + 1) * pts] = v
     for k in range(1, total):
         spread(k).wait_send()
-
-
-def fit_kernel(lhs_ref, rhs_ref, fit_ref, out_ref):
+    keep.wait()
+
+
+def fit_kernel(pieces, lhs_ref, rhs_ref, held_ref, out_hbm, obuf, sems):
     left = jnp.transpose(lhs_ref[...]).astype(BF16)
-    out_ref[...] = fit_ref[...] + dot(left, rhs_ref[...].astype(BF16))
+    right = rhs_ref[...].astype(BF16)
+    step = obuf.shape[0] // pieces
+    copies = []
+    for p in range(pieces):
+        part = pl.ds(p * step, step)
+        obuf[part, :] = held_ref[part, :] + dot(left[p * step:(p + 1) * step], right)
+        copies.append(pltpu.make_async_copy(obuf.at[part], out_hbm.at[part], sems.at[p]))
+        copies[-1].start()
+    for copy in copies:
+        copy.wait()
 
 
 def on_device(ng, nc, chol_block, orbitals, fit_in):
@@ -180,13 +192,14 @@
     total = ng * nc
     dma = pltpu.SemaphoreType.DMA
     vmem = pl.BlockSpec(memory_space=pltpu.VMEM)
-    hbm = pl.BlockSpec(memory_space=pl.ANY)
-    lhs, rhs = pl.pallas_call(
+    hbm = pl.BlockSpec(memory_space=pltpu.HBM)
+    lhs, rhs, held = pl.pallas_call(
         functools.partial(gather_kernel, ng, nc, nch),
         out_shape=(jax.ShapeDtypeStruct((depth, tile_rows), F32),
-                   jax.ShapeDtypeStruct((depth, tile_cols), F32)),
-        in_specs=[hbm, hbm],
-        out_specs=(vmem, vmem),
+                   jax.ShapeDtypeStruct((depth, tile_cols), F32),
+                   jax.ShapeDtypeStruct(fit_in.shape, F32)),
+        in_specs=[hbm, hbm, hbm],
+        out_specs=(vmem, vmem, vmem),
         scratch_shapes=[
             pltpu.VMEM((ng, rows, norb), F32),
             pltpu.VMEM((pts, norb), F32),
@@ -195,7 +208,7 @@
             pltpu.VMEM((norb, pts), BF16),
             pltpu.VMEM((8, pts), F32),
             pltpu.VMEM((total, 1, pts), F32),
-            dma, dma,
+            dma, dma, dma,
             dma((nch, chips)), dma((nch, chips)),
             dma((nch, chips)), dma((nch, chips)),
             dma((total,)), dma((total,)),
@@ -203,20 +216,17 @@
         compiler_params=pltpu.CompilerParams(
             collective_id=0, has_side_effects=True, vmem_limit_bytes=40 << 20),
         name="gather",
-    )(chol_block, orbitals)
-    tile = min(256, tile_rows)
+    )(*(pltpu.with_memory_space_constraint(a, pltpu.HBM) for a in (chol_block, orbitals, fit_in)))
+    pieces = 8
     return pl.pallas_call(
-        fit_kernel,
-        grid=(tile_rows // tile,),
+        functools.partial(fit_kernel, pieces),
         out_shape=jax.ShapeDtypeStruct(fit_in.shape, F32),
-        in_specs=[
-            pl.BlockSpec((depth, tile), lambda r: (0, r)),
-            pl.BlockSpec((depth, tile_cols), lambda r: (0, 0)),
-            pl.BlockSpec((tile, tile_cols), lambda r: (r, 0)),
-        ],
-        out_specs=pl.BlockSpec((tile, tile_cols), lambda r: (r, 0)),
+        in_specs=[vmem, vmem, vmem],
+        out_specs=hbm,
+        scratch_shapes=[pltpu.VMEM(fit_in.shape, F32), dma((pieces,))],
+        compiler_params=pltpu.CompilerParams(vmem_limit_bytes=20 << 20),
         name="fit",
-    )(lhs, rhs, fit_in)
+    )(lhs, rhs, held)
 
 
 def solution(mesh):

time: 48.3 us -> 40.3 us (0.83)
  local copies, waits for them, and re-layouts: 4.68 us -> 0 us
  Pallas kernels: 43.3 us -> 40.1 us
    unnamed x8 -> x0, local copies, waits for them, and re-layouts: 4.68 us -> none
    pallas_call x1, Pallas kernels: 5.27 us -> 2.35 us  [on_device(): pl.pallas_call(functools.partial(fit_kernel, pieces), out_shape=jax.Shape...]
where the time goes in v2:
time: 40.3 us; the launch traced here: 40.2 us
  Pallas kernels  40.1 us (100%)
    pallas_call x1, Pallas kernels, on_device(): pl.pallas_call(functools.partial(gather_kernel, ng, nc, nch), out_shape=(...  37.8 us
    pallas_call x1, Pallas kernels, on_device(): pl.pallas_call(functools.partial(fit_kernel, pieces), out_shape=jax.Shape...  2.35 us

profile of v2, /device:TPU:0, one launch (start us, length us, event | category | flops | bytes accessed | tf_op | source)
XLA Modules:
  0.0 40.2 jit_solution(1601919288784515071)
XLA Ops:
  0.0 37.8 %gather.1 = (f32[24,1024]{1,0:T(8,128)S(1)}, f32[24,1024]{1,0:T(8,128)S(1)}, f32[1024,1024]{1,0:T(8,128)S(1)}) custom-call(f32[1,256,1024]{2,1,0:T(8,128)} %chol_hbm.1, f32[1024,1024]{1,0:T(8,128)} %orb_hbm.1, f32[1024,1024]{1,0:T(8,128)} %fit_hbm.1), custom_call_target="tpu_custom_call" | custom-call | tf_op jit(solution)/shard_map/gather/pallas_call | solution.py:196
  37.8 2.4 %fit.1 = f32[1024,1024]{1,0:T(8,128)} custom-call(f32[24,1024]{1,0:T(8,128)S(1)} %get-tuple-element.8.lhs_ref, f32[24,1024]{1,0:T(8,128)S(1)} %get-tuple-element.9.rhs_ref, f32[1024,1024]{1,0:T(8,128)S(1)} %get-tuple-element.10.held_ref), custom_call_target="tpu_custom_call" | custom-call | tf_op jit(solution)/shard_map/fit/pallas_call | solution.py:221

commit v3 on v2

v3 whole, which is shorter than its diff:
```python
import functools

import jax
import jax.numpy as jnp
from jax import lax
from jax.experimental import pallas as pl
from jax.experimental.pallas import tpu as pltpu
from jax.sharding import PartitionSpec as P

MESH = pl.DeviceIdType.MESH
F32 = jnp.float32
BF16 = jnp.bfloat16


def split2(a):
    hi = a.astype(BF16)
    return hi, (a - hi.astype(F32)).astype(BF16)


def dot(a, b):
    return jnp.dot(a, b, preferred_element_type=F32)


TILE = 256


class Place:
    def __init__(self, ng, nc):
        self.ng, self.nc, self.total, self.chips = ng, nc, ng * nc, ng // 2
        self.g = lax.axis_index("groups")
        self.i = lax.axis_index("grid")
        self.c = lax.axis_index("chol")
        self.core = lax.rem(self.i, 2)
        self.chip = lax.div(self.i, 2)
        self.sib = self.i + 1 - 2 * self.core
        self.flat = self.i * nc + self.c

    def peer(self, k):
        t = lax.rem(self.flat + k, self.total)
        return (self.g, lax.div(t, self.nc), lax.rem(t, self.nc))

    def greet(self):
        barrier = pltpu.get_barrier_semaphore()
        for k in range(1, self.total):
            pl.semaphore_signal(barrier, inc=1, device_id=self.peer(k), device_id_type=MESH)
        pl.semaphore_wait(barrier, self.total - 1)

    def send(self, src, dst, send_sem, recv_sem, to):
        return pltpu.make_async_remote_copy(
            src_ref=src, dst_ref=dst, send_sem=send_sem, recv_sem=recv_sem,
            device_id=(self.g, to, self.c), device_id_type=MESH)


def turn(xbuf, xt, xth, xtl):
    pts = xbuf.shape[0]
    tile = min(256, pts)

    @pl.loop(0, pts // tile)
    def _(p):
        at = pl.multiple_of(p * tile, tile)
        block = jnp.transpose(xbuf[pl.ds(at, tile), :])
        xt[:, pl.ds(at, tile)] = block
        hi, lo = split2(block)
        xth[:, pl.ds(at, tile)] = hi
        xtl[:, pl.ds(at, tile)] = lo


def add(acc, xt, xth, xtl, block, base, spans):
    count = block.shape[0]
    pts = xt.shape[1]
    tile = min(TILE, pts)
    hi, lo = split2(block)
    both = jnp.concatenate([hi, lo], axis=0)

    @pl.loop(0, pts // tile)
    def _(p):
        at = pl.multiple_of(p * tile, tile)
        cols = pl.ds(at, tile)
        half = None
        for first, where, width in spans:
            k = pl.ds(pl.multiple_of(where, 16), width)
            two = dot(both[:, first:first + width], xth[k, cols])
            term = two[:count] + (two[count:] + dot(hi[:, first:first + width], xtl[k, cols]))
            half = term if half is None else half + term
        prod = half * xt[pl.ds(pl.multiple_of(base, 8), count), cols]
        acc[:, cols] += jnp.sum(prod.reshape(count // 8, 8, tile), axis=0)


def finish(at, acc, allc, lhs_ref, rhs_ref, csend, crecv, drain):
    nc, total, pts = at.nc, at.total, allc.shape[2]
    allc[at.flat] = jnp.sum(acc[...], axis=0, keepdims=True)

    def spread(k):
        return pltpu.make_async_remote_copy(
            src_ref=allc.at[at.flat], dst_ref=allc.at[at.flat],
            send_sem=csend.at[k], recv_sem=crecv.at[k],
            device_id=at.peer(k), device_id_type=MESH)

    for k in range(1, total):
        spread(k).start()
    lhs_ref[...] = jnp.zeros_like(lhs_ref)
    rhs_ref[...] = jnp.zeros_like(rhs_ref)
    drain()
    for k in range(1, total):
        back = lax.rem(at.flat - k + total, total)
        pltpu.make_async_remote_copy(
            src_ref=allc.at[back], dst_ref=allc.at[back],
            send_sem=csend.at[k], recv_sem=crecv.at[k],
            device_id=(at.g, at.i, at.c), device_id_type=MESH).wait_recv()

    def terms(v):
        h = v.astype(BF16).astype(F32)
        r = v - h
        m = r.astype(BF16).astype(F32)
        return h, m, (r - m).astype(BF16).astype(F32)

    blocks = lhs_ref.shape[1] // pts
    for n in range(nc):
        h, m, l = terms(allc[at.i * nc + n])
        for t, v in enumerate((h, m, h, l, h, m)):
            rhs_ref[t * nc + n:t * nc + n + 1, :] = v
        for b in range(blocks):
            h, m, l = terms(allc[(at.c * blocks + b) * nc + n])
            for t, v in enumerate((h, h, m, h, l, m)):
                lhs_ref[t * nc + n:t * nc + n + 1, b * pts:(b + 1) * pts] = v
    for k in range(1, total):
        spread(k).wait_send()


def begin(at, chol_hbm, orb_hbm, fit_hbm, held_ref, mine, xbuf, sems):
    copies = [pltpu.make_async_copy(chol_hbm.at[0], mine, sems.at[0]),
              pltpu.make_async_copy(orb_hbm, xbuf, sems.at[1]),
              pltpu.make_async_copy(fit_hbm, held_ref, sems.at[2])]
    copies[0].start()
    copies[1].start()
    at.greet()
    return copies


def pair_kernel(ng, nc, nch, chol_hbm, orb_hbm, fit_hbm, lhs_ref, rhs_ref, held_ref,
                lbuf, obuf, dsend, esend, dbuf, ebuf, xbuf, xt, xth, xtl, acc, allc,
                sems, ysend, yrecv, ssend, srecv, csend, crecv):
    at = Place(ng, nc)
    rows = lbuf.shape[1]
    half, step, wide = rows // 2, rows // nch, 2 * rows
    core, other = at.core, 1 - at.core
    away = (1 - at.chip) * 2 + core
    pieces = nch + 2
    own, xcopy, keep = begin(at, chol_hbm, orb_hbm, fit_hbm, held_ref, lbuf.at[core], xbuf, sems)
    far = pl.ds(pl.multiple_of((1 - at.chip) * wide, 128), wide)

    def slot(p, s):
        if p < nch:
            return obuf.at[s, pl.ds(p * step, step)]
        return (dbuf if p == nch else ebuf).at[s]

    def over(p):
        if p < nch:
            src = chol_hbm.at[0, pl.ds(p * step, step), far]
        else:
            src = dsend if p == nch else esend
        return at.send(src, slot(p, core), ysend.at[p], yrecv.at[p], away)

    def forward(p):
        return at.send(slot(p, core), slot(p, core), ssend.at[p], srecv.at[p], at.sib)

    for p in range(nch):
        over(p).start()
    home = at.send(chol_hbm.at[0], lbuf.at[core], ssend.at[pieces], srecv.at[pieces], at.sib)
    home.start()
    xcopy.wait()
    turn(xbuf, xt, xth, xtl)
    acc[...] = jnp.zeros_like(acc)

    own.wait()
    home.wait_recv()
    mine = pl.multiple_of(at.i * rows, 128)
    theirs = pl.multiple_of(at.sib * rows, 128)

    def both_ways(h):
        k = core + h - 2 * core * h
        one = lbuf[core, h * half:(h + 1) * half, pl.ds(pl.multiple_of(theirs + k * half, 128), half)]
        two = lbuf[other, pl.ds(pl.multiple_of(k * half, 8), half), pl.ds(pl.multiple_of(mine + h * half, 128), half)]
        return one + jnp.transpose(two)

    left = pl.ds(mine, half)
    right = pl.ds(pl.multiple_of(mine + half, 128), half)
    dsend[:, :half] = lbuf[core, :half, left]
    dsend[:, half:2 * half] = lbuf[core, :half, right] + jnp.transpose(lbuf[core, half:, left])
    dsend[:, 2 * half:] = both_ways(0)
    esend[:, :half] = lbuf[core, half:, right]
    esend[:, half:] = both_ways(1)
    over(nch).start()
    over(nch + 1).start()
    keep.start()

    put = functools.partial(add, acc, xt, xth, xtl)
    norb = lbuf.shape[2]
    put(lbuf[core], mine, [(0, 0, norb)])
    put(lbuf[other], theirs, [(0, 0, norb)])

    def take(p, s):
        src = ((1 - at.chip) * 2 + s) * rows
        sib = ((1 - at.chip) * 2 + 1 - s) * rows
        if p < nch:
            put(obuf[s, p * step:(p + 1) * step], src + p * step, [(0, at.chip * wide, wide)])
        elif p == nch:
            put(dbuf[s], src, [(0, src, 2 * half), (2 * half, sib + s * half, half)])
        else:
            put(ebuf[s], src + half, [(0, src + half, half), (half, sib + (1 - s) * half, half)])

    for p in range(pieces):
        over(p).wait_recv()
        forward(p).start()
        take(p, core)
        forward(p).wait_recv()
        take(p, other)

    def drain():
        home.wait_send()
        for p in range(pieces):
            over(p).wait_send()
            forward(p).wait_send()
        keep.wait()

    finish(at, acc, allc, lhs_ref, rhs_ref, csend, crecv, drain)


def ring_kernel(ng, nc, nch, chol_hbm, orb_hbm, fit_hbm, lhs_ref, rhs_ref, held_ref,
                lbuf, xbuf, xt, xth, xtl, acc, allc,
                sems, ysend, yrecv, ssend, srecv, csend, crecv):
    at = Place(ng, nc)
    rows, norb = lbuf.shape[1:]
    step = rows // nch
    own, xcopy, keep = begin(at, chol_hbm, orb_hbm, fit_hbm, held_ref, lbuf.at[at.i], xbuf, sems)

    def over(ch, d):
        part = pl.ds(ch * step, step)
        to = lax.rem(at.chip + d, at.chips) * 2 + at.core
        return at.send(chol_hbm.at[0, part], lbuf.at[at.i, part], ysend.at[ch, d], yrecv.at[ch, d], to)

    def source(d):
        return lax.rem(at.chip - d + at.chips, at.chips) * 2 + at.core

    def forward(ch, d):
        ref = lbuf.at[source(d), pl.ds(ch * step, step)]
        return at.send(ref, ref, ssend.at[ch, d], srecv.at[ch, d], at.sib)

    for ch in range(nch):
        for d in range(1, at.chips):
            over(ch, d).start()
    home = at.send(chol_hbm.at[0], lbuf.at[at.i], ssend.at[0, 0], srecv.at[0, 0], at.sib)
    home.start()
    keep.start()
    xcopy.wait()
    turn(xbuf, xt, xth, xtl)
    acc[...] = jnp.zeros_like(acc)

    def put(src, first, count):
        add(acc, xt, xth, xtl, lbuf[src, pl.ds(first, count), :], src * rows + first, [(0, 0, norb)])

    own.wait()
    put(at.i, 0, rows)
    home.wait()
    put(at.sib, 0, rows)
    for ch in range(nch):
        for d in range(1, at.chips):
            src = source(d)
            over(ch, d).wait_recv()
            forward(ch, d).start()
            put(src, ch * step, step)
            forward(ch, d).wait_recv()
            put(src + 1 - 2 * at.core, ch * step, step)

    def drain():
        for ch in range(nch):
            for d in range(1, at.chips):
                over(ch, d).wait_send()
                forward(ch, d).wait_send()
        keep.wait()

    finish(at, acc, allc, lhs_ref, rhs_ref, csend, crecv, drain)


def fit_kernel(pieces, lhs_ref, rhs_ref, held_ref, out_hbm, obuf, sems):
    left = jnp.transpose(lhs_ref[...]).astype(BF16)
    right = rhs_ref[...].astype(BF16)
    step = obuf.shape[0] // pieces
    copies = []
    for p in range(pieces):
        part = pl.ds(p * step, step)
        obuf[part, :] = held_ref[part, :] + dot(left[p * step:(p + 1) * step], right)
        copies.append(pltpu.make_async_copy(obuf.at[part], out_hbm.at[part], sems.at[p]))
        copies[-1].start()
    for copy in copies:
        copy.wait()


def on_device(ng, nc, chol_block, orbitals, fit_in):
    rows, norb = chol_block.shape[1:]
    pts = orbitals.shape[0]
    tile_rows, tile_cols = fit_in.shape
    chips = ng // 2
    depth = -(-6 * nc // 8) * 8
    total = ng * nc
    dma = pltpu.SemaphoreType.DMA
    vmem = pl.BlockSpec(memory_space=pltpu.VMEM)
    hbm = pl.BlockSpec(memory_space=pltpu.HBM)
    if chips == 2 and rows % 256 == 0:
        kernel, nch, half = pair_kernel, 2, rows // 2
        blocks = [(2, rows, norb), (2, rows, 2 * rows), (half, 3 * half), (half, 2 * half),
                  (2, half, 3 * half), (2, half, 2 * half)]
        links = [dma((nch + 2,)), dma((nch + 2,)), dma((nch + 3,)), dma((nch + 3,))]
    else:
        kernel, nch = ring_kernel, 4
        blocks = [(ng, rows, norb)]
        links = [dma((nch, chips))] * 4
    lhs, rhs, held = pl.pallas_call(
        functools.partial(kernel, ng, nc, nch),
        out_shape=(jax.ShapeDtypeStruct((depth, tile_rows), F32),
                   jax.ShapeDtypeStruct((depth, tile_cols), F32),
                   jax.ShapeDtypeStruct(fit_in.shape, F32)),
        in_specs=[hbm, hbm, hbm],
        out_specs=(vmem, vmem, vmem),
        scratch_shapes=[
            *(pltpu.VMEM(shape, F32) for shape in blocks),
            pltpu.VMEM((pts, norb), F32),
            pltpu.VMEM((norb, pts), F32),
            pltpu.VMEM((norb, pts), BF16),
            pltpu.VMEM((norb, pts), BF16),
            pltpu.VMEM((8, pts), F32),
            pltpu.VMEM((total, 1, pts), F32),
            dma((3,)), *links,
            dma((total,)), dma((total,)),
        ],
        compiler_params=pltpu.CompilerParams(
            collective_id=0, has_side_effects=True, vmem_limit_bytes=40 << 20),
        name="gather",
    )(*(pltpu.with_memory_space_constraint(a, pltpu.HBM) for a in (chol_block, orbitals, fit_in)))
    pieces = 8
    return pl.pallas_call(
        functools.partial(fit_kernel, pieces),
        out_shape=jax.ShapeDtypeStruct(fit_in.shape, F32),
        in_specs=[vmem, vmem, vmem],
        out_specs=hbm,
        scratch_shapes=[pltpu.VMEM(fit_in.shape, F32), dma((pieces,))],
        compiler_params=pltpu.CompilerParams(vmem_limit_bytes=20 << 20),
        name="fit",
    )(lhs, rhs, held)


def solution(mesh):
    placed = (
        P(("groups", "chol"), "grid", None),
        P(("groups", "grid"), None),
        P(("groups", "chol"), "grid"),
    )
    return jax.shard_map(
        functools.partial(on_device, mesh.shape["grid"], mesh.shape["chol"]),
        mesh=mesh,
        in_specs=placed,
        out_specs=P(("groups", "chol"), "grid"),
        check_vma=False,
    )
```

time: 40.3 us -> 35 us (0.87)
  Pallas kernels: 40.1 us -> 34.9 us
    pallas_call x1, Pallas kernels: 37.8 us -> 32.5 us  [on_device(): pl.pallas_call(functools.partial(kernel, ng, nc, nch), out_shape=(jax.Sha...]
where the time goes in v3:
time: 35 us; the launch traced here: 34.9 us
  Pallas kernels  34.9 us (100%)
    pallas_call x1, Pallas kernels, on_device(): pl.pallas_call(functools.partial(kernel, ng, nc, nch), out_shape=(jax.Sha...  32.5 us
    pallas_call x1, Pallas kernels, on_device(): pl.pallas_call(functools.partial(fit_kernel, pieces), out_shape=jax.Shape...  2.34 us

profile of v3, /device:TPU:0, one launch (start us, length us, event | category | flops | bytes accessed | tf_op | source)
XLA Modules:
  0.0 34.9 jit_solution(14475769518025970027)
XLA Ops:
  0.0 32.5 %gather.1 = (f32[24,1024]{1,0:T(8,128)S(1)}, f32[24,1024]{1,0:T(8,128)S(1)}, f32[1024,1024]{1,0:T(8,128)S(1)}) custom-call(f32[1,256,1024]{2,1,0:T(8,128)} %chol_hbm.1, f32[1024,1024]{1,0:T(8,128)} %orb_hbm.1, f32[1024,1024]{1,0:T(8,128)} %fit_hbm.1), custom_call_target="tpu_custom_call" | custom-call | tf_op jit(solution)/shard_map/gather/pallas_call | solution.py:318
  32.5 2.3 %fit.1 = f32[1024,1024]{1,0:T(8,128)} custom-call(f32[24,1024]{1,0:T(8,128)S(1)} %get-tuple-element.8.lhs_ref, f32[24,1024]{1,0:T(8,128)S(1)} %get-tuple-element.9.rhs_ref, f32[1024,1024]{1,0:T(8,128)S(1)} %get-tuple-element.10.held_ref), custom_call_target="tpu_custom_call" | custom-call | tf_op jit(solution)/shard_map/fit/pallas_call | solution.py:341

commit v4 on v3

--- a/solution.py
+++ b/solution.py
@@ -21,7 +21,7 @@
     return jnp.dot(a, b, preferred_element_type=F32)
 
 
-TILE = 256
+TILE = 1024
 
 
 class Place:
@@ -87,26 +87,42 @@
 
 
 def finish(at, acc, allc, lhs_ref, rhs_ref, csend, crecv, drain):
-    nc, total, pts = at.nc, at.total, allc.shape[2]
+    nc, pts = at.nc, allc.shape[2]
     allc[at.flat] = jnp.sum(acc[...], axis=0, keepdims=True)
 
-    def spread(k):
+    blocks = lhs_ref.shape[1] // pts
+    mine = allc.at[at.flat]
+
+    def push(slot, index, i, c):
         return pltpu.make_async_remote_copy(
-            src_ref=allc.at[at.flat], dst_ref=allc.at[at.flat],
-            send_sem=csend.at[k], recv_sem=crecv.at[k],
-            device_id=at.peer(k), device_id_type=MESH)
-
-    for k in range(1, total):
-        spread(k).start()
+            src_ref=mine, dst_ref=mine, send_sem=csend.at[slot], recv_sem=crecv.at[index],
+            device_id=(at.g, i, c), device_id_type=MESH)
+
+    def pull(j, n, index):
+        theirs = allc.at[j * nc + n]
+        return pltpu.make_async_remote_copy(
+            src_ref=theirs, dst_ref=theirs, send_sem=csend.at[0], recv_sem=crecv.at[index],
+            device_id=(at.g, at.i, at.c), device_id_type=MESH)
+
+    first = blocks * nc
+    home = lax.div(at.i, blocks)
+    slot = lax.rem(at.i, blocks) * nc + at.c
+    pushes = [push(k - 1, first + k - 1, at.i, lax.rem(at.c + k, nc)) for k in range(1, nc)]
+    pushes += [push(nc - 1 + k - 1, slot, lax.rem(at.i + k, at.ng), home) for k in range(1, at.ng)]
+    for copy in pushes:
+        copy.start()
     lhs_ref[...] = jnp.zeros_like(lhs_ref)
     rhs_ref[...] = jnp.zeros_like(rhs_ref)
     drain()
-    for k in range(1, total):
-        back = lax.rem(at.flat - k + total, total)
-        pltpu.make_async_remote_copy(
-            src_ref=allc.at[back], dst_ref=allc.at[back],
-            send_sem=csend.at[k], recv_sem=crecv.at[k],
-            device_id=(at.g, at.i, at.c), device_id_type=MESH).wait_recv()
+    for k in range(1, nc):
+        pull(at.i, lax.rem(at.c - k + nc, nc), first + k - 1).wait_recv()
+    for b in range(blocks):
+        j = at.c * blocks + b
+
+        @pl.when(j != at.i)
+        def _():
+            for n in range(nc):
+                pull(j, n, b * nc + n).wait_recv()
 
     def terms(v):
         h = v.astype(BF16).astype(F32)
@@ -114,7 +130,6 @@
         m = r.astype(BF16).astype(F32)
         return h, m, (r - m).astype(BF16).astype(F32)
 
-    blocks = lhs_ref.shape[1] // pts
     for n in range(nc):
         h, m, l = terms(allc[at.i * nc + n])
         for t, v in enumerate((h, m, h, l, h, m)):
@@ -123,8 +138,8 @@
             h, m, l = terms(allc[(at.c * blocks + b) * nc + n])
             for t, v in enumerate((h, h, m, h, l, m)):
                 lhs_ref[t * nc + n:t * nc + n + 1, b * pts:(b + 1) * pts] = v
-    for k in range(1, total):
-        spread(k).wait_send()
+    for copy in pushes:
+        copy.wait_send()
 
 
 def begin(at, chol_hbm, orb_hbm, fit_hbm, held_ref, mine, xbuf, sems):
@@ -331,7 +346,7 @@
             pltpu.VMEM((8, pts), F32),
             pltpu.VMEM((total, 1, pts), F32),
             dma((3,)), *links,
-            dma((total,)), dma((total,)),
+            dma((ng + nc,)), dma(((tile_rows // pts + 1) * nc,)),
         ],
         compiler_params=pltpu.CompilerParams(
             collective_id=0, has_side_effects=True, vmem_limit_bytes=40 << 20),

time: 35 us -> 32.5 us (0.929)
  Pallas kernels: 34.9 us -> 32.4 us
    pallas_call x1, Pallas kernels: 32.5 us -> 30 us  [on_device(): pl.pallas_call(functools.partial(kernel, ng, nc, nch), out_shape=(jax.Sha...]
where the time goes in v4:
time: 32.5 us; the launch traced here: 32.4 us
  Pallas kernels  32.4 us (100%)
    pallas_call x1, Pallas kernels, on_device(): pl.pallas_call(functools.partial(kernel, ng, nc, nch), out_shape=(jax.Sha...  30 us
    pallas_call x1, Pallas kernels, on_device(): pl.pallas_call(functools.partial(fit_kernel, pieces), out_shape=jax.Shape...  2.35 us

profile of v4, /device:TPU:0, one launch (start us, length us, event | category | flops | bytes accessed | tf_op | source)
XLA Modules:
  0.0 32.4 jit_solution(2862675532600818679)
XLA Ops:
  0.0 30.0 %gather.1 = (f32[24,1024]{1,0:T(8,128)S(1)}, f32[24,1024]{1,0:T(8,128)S(1)}, f32[1024,1024]{1,0:T(8,128)S(1)}) custom-call(f32[1,256,1024]{2,1,0:T(8,128)} %chol_hbm.1, f32[1024,1024]{1,0:T(8,128)} %orb_hbm.1, f32[1024,1024]{1,0:T(8,128)} %fit_hbm.1), custom_call_target="tpu_custom_call" | custom-call | tf_op jit(solution)/shard_map/gather/pallas_call | solution.py:333
  30.1 2.4 %fit.1 = f32[1024,1024]{1,0:T(8,128)} custom-call(f32[24,1024]{1,0:T(8,128)S(1)} %get-tuple-element.8.lhs_ref, f32[24,1024]{1,0:T(8,128)S(1)} %get-tuple-element.9.rhs_ref, f32[1024,1024]{1,0:T(8,128)S(1)} %get-tuple-element.10.held_ref), custom_call_target="tpu_custom_call" | custom-call | tf_op jit(solution)/shard_map/fit/pallas_call | solution.py:356
